TPU v7x, 32 devices: a whole 2x2x4 slice. The times are simulated.
32 devices in a mesh: scene: 4 (over x, core), view: 4 (over z), half: 2 (over y).
Axes of the slice: x: 2, y: 2, z: 4, core: 2. Of those that a mesh axis runs over, the one named last changes fastest.
Arguments:
- tokens: bfloat16 [16, 512, 2048], P(('scene', 'view'), 'half'), parts along dimension 0, may hold values from -9 to 12
- w_qkv: bfloat16 [2048, 768], replicated, may hold values from -0.125 to 0.125
- w_out: bfloat16 [256, 2048], replicated, may hold values from -5 to 5
- key_lists: int32 [16, 4, 2], P(('scene', 'view'), 'half'), parts along dimension 0, may hold values from 0 to 15, as said below
- list_len: int32 [16, 4], P(('scene', 'view'), 'half'), parts along dimension 0, may hold values from 1 to 2, as said below
Outputs:
- mixed: bfloat16 [16, 512, 2048], P(('scene', 'view'), 'half'), parts along dimension 0
There are 4 independent parts, one for each index of `scene`. A program takes and returns all parts, laid end to end along the dimension named above; an argument that names none is the same for every part. Nothing has to cross between parts.
Inputs may be any that keep to these rules, and one draw needn't show every extreme that they name: `key_lists`: entries of one list are distinct block ids of the scene. `list_len`: some query block lists 2 blocks in every scene.
All inputs are finite; a program needn't handle non-finite values.
Results may differ from a plain program's by a relative error of at most 0.014.
The roundings to bfloat16 on the way count: a program that leaves them out, or rounds other values in their place, can miss the bound.
Values may be sent and summed in bfloat16 or wider, within the bound.
A program may use at most 64 MiB of HBM per device.

v0:
```python
import jax
import jax.numpy as jnp
from jax import lax
from jax.sharding import PartitionSpec as P

HEADS = 4
NEG = -1e30


def block_mask(lists, lengths, count, block):
    key_rows = jnp.arange(count, dtype=jnp.int32)
    key_block = key_rows // block
    slots = jnp.arange(lists.shape[1], dtype=jnp.int32)
    live = slots[None, :] < lengths[:, None]
    hits = (lists[:, :, None] == key_block[None, None, :]) & live[:, :, None]
    return jnp.any(hits, axis=1)


def attend(state, queries, keys, values, allowed):
    peak, total, accum = state
    heads = accum.shape[1]
    q3 = queries.reshape(queries.shape[0], heads, -1)
    k3 = keys.reshape(keys.shape[0], heads, -1)
    v3 = values.reshape(values.shape[0], heads, -1)
    scores = jnp.einsum("qhd,khd->hqk", q3, k3, preferred_element_type=jnp.float32) * q3.shape[
        2
    ] ** (-0.5)
    masked = jnp.where(allowed[None], scores, NEG)
    fresh = jnp.maximum(peak, jnp.max(masked, axis=2))
    weights = jnp.where(allowed[None], jnp.exp(scores - fresh[:, :, None]), 0.0)
    factor = jnp.exp(peak - fresh)
    total = jnp.sum(weights, axis=2)
    summed = jnp.einsum(
        "hqk,khd->qhd", weights.astype(jnp.bfloat16), v3, preferred_element_type=jnp.float32
    )
    accum = accum * factor.T[:, :, None] + summed
    return (fresh, total, accum)


def visit(state, queries, keys, values, allowed):
    return lax.cond(
        jnp.any(allowed),
        lambda held: attend(held, queries, keys, values, allowed),
        lambda held: held,
        state,
    )


def per_device(tokens, w_qkv, w_out, key_lists, list_len):
    rows = tokens.shape[1]
    width = tokens.shape[2]
    flat = tokens.reshape(rows, width)
    inner = w_out.shape[0]
    head_size = inner // HEADS
    proj = jnp.dot(flat, w_qkv, preferred_element_type=jnp.float32).astype(jnp.bfloat16)
    queries = proj[:, :inner]
    keys = proj[:, inner : 2 * inner]
    values = proj[:, 2 * inner :]
    lists = key_lists.reshape(-1, key_lists.shape[2])
    lengths = list_len.reshape(-1)
    local_blocks = lists.shape[0]
    block = rows // local_blocks
    peak0 = jnp.full((HEADS, rows), NEG, jnp.float32)
    total0 = jnp.zeros((HEADS, rows), jnp.float32)
    accum0 = jnp.zeros((rows, HEADS, head_size), jnp.float32)
    view_keys, view_values = (
        lax.all_gather(keys, "half", axis=0, tiled=True),
        lax.all_gather(values, "half", axis=0, tiled=True),
    )
    piece = (
        lax.all_gather(view_keys, "view", axis=0, tiled=True),
        lax.all_gather(view_values, "view", axis=0, tiled=True),
    )
    count = piece[0].shape[0]
    allowed = jnp.repeat(block_mask(lists, lengths, count, block), block, axis=0)
    peak, total, accum = visit((peak0, total0, accum0), queries, piece[0], piece[1], allowed)
    attn = (accum / total.T[:, :, None]).reshape(rows, inner).astype(jnp.bfloat16)
    mixed = jnp.dot(attn, w_out, preferred_element_type=jnp.float32).astype(jnp.bfloat16)
    return mixed.reshape(1, rows, width)


def solution(mesh):
    placed = (
        P(("scene", "view"), "half", None),
        P(),
        P(),
        P(("scene", "view"), "half", None),
        P(("scene", "view"), "half"),
    )
    return jax.shard_map(
        per_device,
        mesh=mesh,
        in_specs=placed,
        out_specs=P(("scene", "view"), "half", None),
        check_vma=False,
    )
```

profile of v0, /device:TPU:0, one launch (start us, length us, event | category | flops | bytes accessed | tf_op | source)
XLA Modules:
  0.0 109.8 jit_solution(13672634810469193445)
XLA Ops:
  6.5 0.0 copy-start
  6.5 0.0 all-gather.3.cloned.1.call-start
  6.5 1.9 %copy-done = bf16[2048,768]{1,0:T(8,128)(2,1)S(1)} copy-done((bf16[2048,768]{1,0:T(8,128)(2,1)S(1)}, bf16[2048,768]{1,0:T(8,128)(2,1)}, u32[]{:S(2)}) %copy-start) | copy-done | bytes 3145752
  8.4 2.2 %convolution_convert_fusion.1 = bf16[256,768]{1,0:T(8,128)(2,1)S(1)} fusion(bf16[2048,768]{1,0:T(8,128)(2,1)S(1)} %copy-done, bf16[1,256,2048]{2,1,0:T(8,128)(2,1)} %param.7), kind=kOutput, calls=%fused_computation.14 | convolution fusion | flops 805502976 | bytes 4587520 | tf_op jit(solution)/shard_map/dot_general | solution.py:55
  10.6 0.7 fusion.18
  11.3 7.2 %all_gather.12 = bf16[512,256]{1,0:T(8,128)(2,1)} all-gather(bf16[256,256]{1,0:T(8,128)(2,1)S(1)} %get-tuple-element.35), channel_id=1, replica_groups=mesh['scene'=4,'view'=4,'half'=2] {'half'}, dimensions={0}, use_global_device_ids=true | all-gather | bytes 393216 | tf_op jit(solution)/shard_map/all_gather | solution.py:67
  18.5 0.0 all-gather.3.cloned.1.call-update
  18.6 0.0 all-gather.5.cloned.1.call-start
  18.6 7.2 %all_gather.14 = bf16[512,256]{1,0:T(8,128)(2,1)} all-gather(bf16[256,256]{1,0:T(8,128)(2,1)} %get-tuple-element.34), channel_id=1, replica_groups=mesh['scene'=4,'view'=4,'half'=2] {'half'}, dimensions={0}, use_global_device_ids=true | all-gather | bytes 393216 | tf_op jit(solution)/shard_map/all_gather | solution.py:68
  25.8 0.0 all-gather.5.cloned.1.call-update
  25.9 0.7 iota_compare_fusion
  26.6 0.8 and_reduce_fusion
  27.4 1.2 %broadcast_reduce_fusion = pred[]{:T(512)} fusion(pred[2,2048]{1,0:T(4,128)(4,1)S(1)} %and_reduce_fusion), kind=kLoop, calls=%fused_computation.16 | loop fusion | flops 524287 | bytes 4097 | tf_op jit(solution)/shard_map/reduce_or | solution.py:42
  29.2 19.0 %all-gather.3.cloned.1.call-done = bf16[2048,256]{1,0:T(8,128)(2,1)} async-done(((bf16[512,256]{1,0:T(8,128)(2,1)}), bf16[2048,256]{1,0:T(8,128)(2,1)}) %all-gather.3.cloned.1.call-update) | async-done | bytes 1048592 | tf_op jit(solution)/shard_map/all_gather | solution.py:71
  48.2 28.9 %all-gather.5.cloned.1.call-done = bf16[2048,256]{1,0:T(8,128)(2,1)} async-done(((bf16[512,256]{1,0:T(8,128)(2,1)}), bf16[2048,256]{1,0:T(8,128)(2,1)}) %all-gather.5.cloned.1.call-update) | async-done | bytes 1048592 | tf_op jit(solution)/shard_map/all_gather | solution.py:72
  77.1 1.0 broadcast_in_dim.41
  78.2 22.1 %conditional.1 = (f32[4,256]{1,0:T(4,128)S(1)}, f32[256,4,64]{0,2,1:T(8,128)S(1)}) conditional(s32[]{:T(128)} %convert_element_type.18, () %tuple.13, (pred[2,128,2048]{2,1,0:T(8,128)(4,1)}, bf16[256,768]{1,0:T(8,128)(2,1)S(1)}, bf16[2048,256]{1,0:T(8,128)(2,1)}, bf16[2048,256]{1,0:T(8,128)(2,1)}) %tuple.14), branch_computations={%region_2.3_spmd, %region_3.6_spmd} | conditional | flops 560006144 | bytes 68059184 | solution.py:41
  78.2 2.3 %copy.10 = bf16[2048,256]{0,1:T(8,128)(2,1)} copy(bf16[2048,256]{1,0:T(8,128)(2,1)} %get-tuple-element.28) | data formatting | bytes 2097152 | tf_op jit(solution)/shard_map
  80.4 0.9 copy.9
  81.3 0.9 slice.12
  82.3 6.2 %select_reduce_fusion = (f32[4,256]{1,0:T(4,128)S(1)}, f32[4,256,2048]{2,1,0:T(8,128)}) fusion(pred[256,2048]{1,0:T(8,128)(4,1)} %bitcast, bf16[256,4,64]{0,2,1:T(8,128)(2,1)S(1)} %bitcast.27, bf16[2048,4,64]{0,2,1:T(8,128)(2,1)} %bitcast.25), kind=kOutput, calls=%fused_computation.1 | convolution fusion | flops 274725888 | bytes 10096640 | tf_op jit(solution)/shard_map/cond/branch_1_fun/qhd,khd->hqk/dot_general | solution.py:25
  88.5 2.3 %copy.11 = bf16[2048,256]{0,1:T(8,128)(2,1)} copy(bf16[2048,256]{1,0:T(8,128)(2,1)} %get-tuple-element.29) | data formatting | bytes 2097152 | tf_op jit(solution)/shard_map
  90.8 0.0 copy-start.1
  90.8 5.2 %fusion.8 = f32[256,4,64]{0,2,1:T(8,128)S(1)} fusion(bf16[2048,4,64]{0,2,1:T(8,128)(2,1)} %bitcast.26, f32[4,256,2048]{2,1,0:T(8,128)} %get-tuple-element.33, f32[4,256]{1,0:T(4,128)S(1)} %get-tuple-element.31, pred[256,2048]{1,0:T(8,128)(4,1)} %bitcast, f32[256,4]{0,1:T(4,128)S(1)} %get-tuple-element.30), kind=kOutput, calls=%fused_computation.7 | convolution fusion | flops 276889600 | bytes 10231808 | tf_op jit(solution)/shard_map/cond/branch_1_fun/hqk,khd->qhd/dot_general | solution.py:33
  96.0 1.1 %copy-done.1 = f32[4,256,2048]{2,1,0:T(8,128)S(1)} copy-done((f32[4,256,2048]{2,1,0:T(8,128)S(1)}, f32[4,256,2048]{2,1,0:T(8,128)}, u32[]{:S(2)}) %copy-start.1) | copy-done | bytes 8388632 | tf_op jit(solution)/shard_map/cond
  97.1 3.2 %fusion.1 = f32[4,256]{1,0:T(4,128)S(1)} fusion(f32[4,256,2048]{2,1,0:T(8,128)S(1)} %copy-done.1, f32[4,256]{1,0:T(4,128)S(1)} %get-tuple-element.31, pred[256,2048]{1,0:T(8,128)(4,1)} %bitcast), kind=kLoop, calls=%fused_computation.3 | loop fusion | flops 8387584 | bytes 8921088 | tf_op jit(solution)/shard_map/cond/branch_1_fun/reduce_sum | solution.py:32
  100.3 2.7 %fusion.13 = bf16[1,256,2048]{2,1,0:T(8,128)(2,1)} fusion(bf16[256,256]{0,1:T(8,128)(2,1)S(1)} %bitcast.28, bf16[256,2048]{1,0:T(8,128)(2,1)} %param.9), kind=kOutput, calls=%fused_computation.13 | convolution fusion | flops 268959744 | bytes 2228224 | tf_op jit(solution)/shard_map/dot_general | solution.py:78
  (3 shorter events, 0.0 us)
Async XLA Ops:
  6.5 1.9 %copy-start = (bf16[2048,768]{1,0:T(8,128)(2,1)S(1)}, bf16[2048,768]{1,0:T(8,128)(2,1)}, u32[]{:S(2)}) copy-start(bf16[2048,768]{1,0:T(8,128)(2,1)} %param.8) | copy-start | bytes 9437188
  6.5 41.7 %all-gather.3.cloned.1.call-start = ((), (), s32[]{:S(2)}) async-start(), calls=%async_computation | async-start | bytes 1310720 | tf_op jit(solution)/shard_map/all_gather | solution.py:71
  18.6 58.6 %all-gather.5.cloned.1.call-start = ((), (), s32[]{:S(2)}) async-start(), calls=%async_computation.1 | async-start | bytes 1310720 | tf_op jit(solution)/shard_map/all_gather | solution.py:72
  90.8 6.3 %copy-start.1 = (f32[4,256,2048]{2,1,0:T(8,128)S(1)}, f32[4,256,2048]{2,1,0:T(8,128)}, u32[]{:S(2)}) copy-start(f32[4,256,2048]{2,1,0:T(8,128)} %get-tuple-element.33) | copy-start | bytes 25165828 | tf_op jit(solution)/shard_map/cond
Sparse Core Ops, SparseCore 0:
  18.7 29.4 all-gather.2
  49.8 27.3 all-gather.4
where the time goes:
time: 110 us
  waiting for transfers between devices  47.9 us (44%)
  matrix products  16.3 us (15%)
  blocking collectives  14.4 us (13%)
  between operations  14.1 us (13%)
  local copies, waits for them, and re-layouts  11.1 us (10%)
  other arithmetic  5.97 us (5%)
    all_gather x1, waiting for transfers between devices, per_device(): lax.all_gather(view_values, 'view', axis=0, tiled=True)  28.9 us
    all_gather x1, waiting for transfers between devices, per_device(): lax.all_gather(view_keys, 'view', axis=0, tiled=True)  19 us
    all_gather x1, blocking collectives, per_device(): lax.all_gather(keys, 'half', axis=0, tiled=True)  7.24 us
    all_gather x1, blocking collectives, per_device(): lax.all_gather(values, 'half', axis=0, tiled=True)  7.21 us
    dot_general x1, matrix products, attend(): jnp.einsum('qhd,khd->hqk', q3, k3, preferred_element_type=jnp.float32)  6.24 us
    another operation x3, local copies, waits for them, and re-layouts  5.44 us
    dot_general x1, matrix products, attend(): jnp.einsum('hqk,khd->qhd', weights.astype(jnp.bfloat16), v3, preferred_el...  5.18 us
    reduce_sum x1, other arithmetic, attend(): total = jnp.sum(weights, axis=2)  3.21 us
  transfers between devices with their start and end apart: 2, of which 2 were waited for; matrix products, arithmetic and copies ran while one was open for 2% of the time, Pallas kernels for 0%

commit v1 on v0

--- a/solution.py
+++ b/solution.py
@@ -5,6 +5,27 @@
 
 HEADS = 4
 NEG = -1e30
+
+
+def joined_along(tiles, dim):
+    lengths = list(tiles.shape[1:])
+    lengths[dim] *= tiles.shape[0]
+    return jnp.moveaxis(tiles, 0, dim).reshape(lengths)
+
+
+def grow_blocks(x, axis):
+    peers, position = (lax.axis_size(axis), lax.axis_index(axis))
+    tiles, bit = (x[None], 1)
+    while bit < peers:
+        other = lax.ppermute(tiles, axis, [(i, i ^ bit) for i in range(peers)])
+        low = position & bit == 0
+        tiles = jnp.concatenate([jnp.where(low, tiles, other), jnp.where(low, other, tiles)])
+        bit *= 2
+    return tiles
+
+
+def collect(array, axis, dim):
+    return joined_along(grow_blocks(array, axis), dim)
 
 
 def block_mask(lists, lengths, count, block):
@@ -64,7 +85,7 @@
     total0 = jnp.zeros((HEADS, rows), jnp.float32)
     accum0 = jnp.zeros((rows, HEADS, head_size), jnp.float32)
     view_keys, view_values = (
-        lax.all_gather(keys, "half", axis=0, tiled=True),
+        collect(keys, "half", 0),
         lax.all_gather(values, "half", axis=0, tiled=True),
     )
     piece = (

time: 110 us -> 102 us (0.927)
  blocking collectives: 14.4 us -> 7.24 us
  matrix products: 16.3 us -> 10.9 us
  waiting for transfers between devices: 47.9 us -> 51.2 us
  starting transfers between devices: 0.04 us -> 1.86 us
  local copies, waits for them, and re-layouts: 11.1 us -> 9.55 us
    all_gather x1, waiting for transfers between devices: 28.9 us -> 18.7 us  [per_device(): lax.all_gather(view_values, 'view', axis=0, tiled=True)]
    all_gather x1, waiting for transfers between devices: 19 us -> 29 us  [per_device(): lax.all_gather(view_keys, 'view', axis=0, tiled=True)]
    all_gather x1 -> x0, blocking collectives: 7.24 us -> none  [per_device(): lax.all_gather(keys, 'half', axis=0, tiled=True)]
    ppermute x0 -> x1, waiting for transfers between devices: none -> 3.53 us  [grow_blocks(): other = lax.ppermute(tiles, axis, [(i, i ^ bit) for i in range(peers)])]
    dot_general x1, matrix products: 6.24 us -> 3.14 us  [attend(): jnp.einsum('qhd,khd->hqk', q3, k3, preferred_element_type=jnp.float32)]
    dot_general x1, matrix products: 5.18 us -> 2.87 us  [attend(): jnp.einsum('hqk,khd->qhd', weights.astype(jnp.bfloat16), v3, preferred_el...]
    another operation x3 -> x2, local copies, waits for them, and re-layouts: 5.44 us -> 3.19 us
    ppermute x0 -> x1, starting transfers between devices: none -> 1.82 us  [grow_blocks(): other = lax.ppermute(tiles, axis, [(i, i ^ bit) for i in range(peers)])]
  transfers between devices with their start and end apart: 2 -> 3, of which waited for: 2 -> 3; matrix products, arithmetic and copies ran while one was open for 2% -> 5% of each run, Pallas kernels for 0% -> 0%
where the time goes in v1:
time: 102 us; the launch traced here: 101 us
  waiting for transfers between devices  51.2 us (50%)
  between operations  14.1 us (14%)
  matrix products  10.9 us (11%)
  local copies, waits for them, and re-layouts  9.55 us (9%)
  blocking collectives  7.24 us (7%)
  other arithmetic  6.29 us (6%)
  starting transfers between devices  1.86 us (2%)
    all_gather x1, waiting for transfers between devices, per_device(): lax.all_gather(view_keys, 'view', axis=0, tiled=True)  29 us
    all_gather x1, waiting for transfers between devices, per_device(): lax.all_gather(view_values, 'view', axis=0, tiled=True)  18.7 us
    all_gather x1, blocking collectives, per_device(): lax.all_gather(values, 'half', axis=0, tiled=True)  7.24 us
    ppermute x1, waiting for transfers between devices, grow_blocks(): other = lax.ppermute(tiles, axis, [(i, i ^ bit) for i in range(peers)])  3.53 us
    reduce_sum x1, other arithmetic, attend(): total = jnp.sum(weights, axis=2)  3.22 us
    another operation x2, local copies, waits for them, and re-layouts  3.19 us
    dot_general x1, matrix products, attend(): jnp.einsum('qhd,khd->hqk', q3, k3, preferred_element_type=jnp.float32)  3.14 us
    dot_general x1, matrix products, attend(): jnp.einsum('hqk,khd->qhd', weights.astype(jnp.bfloat16), v3, preferred_el...  2.87 us
  transfers between devices with their start and end apart: 3, of which 3 were waited for; matrix products, arithmetic and copies ran while one was open for 5% of the time, Pallas kernels for 0%

profile of v1, /device:TPU:0, one launch (start us, length us, event | category | flops | bytes accessed | tf_op | source)
XLA Modules:
  0.0 101.2 jit_solution(2738784510463417492)
XLA Ops:
  6.5 0.0 copy-start
  6.5 0.0 copy-start.3
  6.5 0.0 copy-start.2
  6.5 0.0 all-gather.5.cloned.1.call-start
  6.5 1.9 %copy-done = bf16[2048,768]{1,0:T(8,128)(2,1)S(1)} copy-done((bf16[2048,768]{1,0:T(8,128)(2,1)S(1)}, bf16[2048,768]{1,0:T(8,128)(2,1)}, u32[]{:S(2)}) %copy-start) | copy-done | bytes 3145752
  8.4 2.2 %convolution_convert_fusion.1 = bf16[256,768]{1,0:T(8,128)(2,1)S(1)} fusion(bf16[2048,768]{1,0:T(8,128)(2,1)S(1)} %copy-done, bf16[1,256,2048]{2,1,0:T(8,128)(2,1)} %param.7), kind=kOutput, calls=%fused_computation.14 | convolution fusion | flops 805502976 | bytes 4587520 | tf_op jit(solution)/shard_map/dot_general | solution.py:76
  10.6 0.7 fusion.18
  11.3 7.2 %all_gather.10 = bf16[512,256]{1,0:T(8,128)(2,1)} all-gather(bf16[256,256]{1,0:T(8,128)(2,1)S(1)} %get-tuple-element.36), channel_id=1, replica_groups=mesh['scene'=4,'view'=4,'half'=2] {'half'}, dimensions={0}, use_global_device_ids=true | all-gather | bytes 393216 | tf_op jit(solution)/shard_map/all_gather | solution.py:89
  18.5 0.0 all-gather.5.cloned.1.call-update
  18.6 0.0 all-gather.3.cloned.1.call-start
  18.6 1.8 %collective-permute-start = (bf16[1,256,256]{2,1,0:T(8,128)(2,1)}, bf16[1,256,256]{2,1,0:T(8,128)(2,1)}, u32[]{:S(2)}, u32[]{:S(2)}) collective-permute-start(bf16[1,256,256]{2,1,0:T(8,128)(2,1)} %get-tuple-element.37), channel_id=1, source_target_pairs={{0,1},{1,0},{2,3},{3,2},{4,5},{5,4},{6,7},{7,6},{8,9},{9,8},{10,11... | collective-permute-start | bytes 393224 | tf_op jit(solution)/shard_map/ppermute | solution.py:20
  20.4 3.5 %collective-permute-done = bf16[1,256,256]{2,1,0:T(8,128)(2,1)} collective-permute-done((bf16[1,256,256]{2,1,0:T(8,128)(2,1)}, bf16[1,256,256]{2,1,0:T(8,128)(2,1)}, u32[]{:S(2)}, u32[]{:S(2)}) %collective-permute-start) | collective-permute-done | bytes 131104 | tf_op jit(solution)/shard_map/ppermute | solution.py:20
  24.0 0.9 broadcast_select_fusion.1
  24.9 0.7 pad_maximum_fusion
  25.6 1.8 %copy.9 = bf16[512,256]{0,1:T(8,128)(2,1)} copy(bf16[512,256]{1,0:T(8,128)(2,1)} %bitcast.34) | data formatting | bytes 524288 | tf_op jit(solution)/shard_map/reshape | solution.py:13
  27.4 0.0 all-gather.3.cloned.1.call-update
  27.5 0.0 copy-done.3
  27.5 0.1 iota_compare_fusion
  27.5 0.0 copy-done.2
  27.5 0.1 and_reduce_fusion
  27.7 1.2 %broadcast_reduce_fusion = pred[]{:T(512)} fusion(pred[2,2048]{1,0:T(4,128)(4,1)S(1)} %and_reduce_fusion), kind=kLoop, calls=%fused_computation.16 | loop fusion | flops 524287 | bytes 4097 | tf_op jit(solution)/shard_map/reduce_or | solution.py:63
  29.5 18.7 %all-gather.5.cloned.1.call-done = bf16[2048,256]{1,0:T(8,128)(2,1)} async-done(((bf16[512,256]{1,0:T(8,128)(2,1)}), bf16[2048,256]{1,0:T(8,128)(2,1)}) %all-gather.5.cloned.1.call-update) | async-done | bytes 1048592 | tf_op jit(solution)/shard_map/all_gather | solution.py:93
  48.2 29.0 %all-gather.3.cloned.1.call-done = bf16[2048,256]{0,1:T(8,128)(2,1)} async-done(((bf16[512,256]{0,1:T(8,128)(2,1)}), bf16[2048,256]{0,1:T(8,128)(2,1)}) %all-gather.3.cloned.1.call-update) | async-done | bytes 1048592 | tf_op jit(solution)/shard_map/all_gather | solution.py:92
  77.2 1.0 broadcast_in_dim.44
  78.2 13.5 %conditional.1 = (f32[4,256]{1,0:T(4,128)S(1)}, f32[256,4,64]{0,2,1:T(8,128)S(1)}) conditional(s32[]{:T(128)} %convert_element_type.18, () %tuple.13, (pred[2,128,2048]{2,1,0:T(8,128)(4,1)}, bf16[256,768]{1,0:T(8,128)(2,1)S(1)}, bf16[2048,256]{0,1:T(8,128)(2,1)}, bf16[2048,256]{1,0:T(8,128)(2,1)}) %tuple.14), branch_computations={%region_2.3_spmd, %region_3.6_spmd} | conditional | flops 560006144 | bytes 36601900 | solution.py:62
  78.2 2.3 %copy.11 = bf16[2048,256]{0,1:T(8,128)(2,1)} copy(bf16[2048,256]{1,0:T(8,128)(2,1)} %get-tuple-element.29) | data formatting | bytes 2097152 | tf_op jit(solution)/shard_map
  80.4 0.9 copy.10
  81.4 0.0 copy-start.1
  81.4 1.0 slice.12
  82.4 3.1 %select_reduce_fusion = (f32[4,256]{1,0:T(4,128)S(1)}, f32[4,256,2048]{2,1,0:T(8,128)S(1)}) fusion(pred[256,2048]{1,0:T(8,128)(4,1)} %bitcast, bf16[256,4,64]{0,2,1:T(8,128)(2,1)S(1)} %bitcast.35, bf16[2048,4,64]{0,2,1:T(8,128)(2,1)} %bitcast.32), kind=kOutput, calls=%fused_computation.1 | convolution fusion | flops 274725888 | bytes 10096640 | tf_op jit(solution)/shard_map/cond/branch_1_fun/qhd,khd->hqk/dot_general | solution.py:46
  85.5 0.0 copy-done.1
  85.5 2.9 %fusion.8 = f32[256,4,64]{0,2,1:T(8,128)S(1)} fusion(bf16[2048,4,64]{0,2,1:T(8,128)(2,1)S(1)} %bitcast.33, f32[4,256,2048]{2,1,0:T(8,128)S(1)} %get-tuple-element.33, f32[4,256]{1,0:T(4,128)S(1)} %get-tuple-element.31, pred[256,2048]{1,0:T(8,128)(4,1)} %bitcast, f32[256,4]{0,1:T(4,128)S(1)} %get-tuple-element.30), kind=kOutput, calls=%fused_computation.7 | convolution fusion | flops 276889600 | bytes 10231808 | tf_op jit(solution)/shard_map/cond/branch_1_fun/hqk,khd->qhd/dot_general | solution.py:54
  88.4 3.2 %fusion.1 = f32[4,256]{1,0:T(4,128)S(1)} fusion(f32[4,256,2048]{2,1,0:T(8,128)S(1)} %get-tuple-element.33, f32[4,256]{1,0:T(4,128)S(1)} %get-tuple-element.31, pred[256,2048]{1,0:T(8,128)(4,1)} %bitcast), kind=kLoop, calls=%fused_computation.3 | loop fusion | flops 8387584 | bytes 8921088 | tf_op jit(solution)/shard_map/cond/branch_1_fun/reduce_sum | solution.py:53
  91.7 2.7 %fusion.13 = bf16[1,256,2048]{2,1,0:T(8,128)(2,1)} fusion(bf16[256,256]{0,1:T(8,128)(2,1)S(1)} %bitcast.36, bf16[256,2048]{1,0:T(8,128)(2,1)} %param.9), kind=kOutput, calls=%fused_computation.13 | convolution fusion | flops 268959744 | bytes 2228224 | tf_op jit(solution)/shard_map/dot_general | solution.py:99
  (3 shorter events, 0.0 us)
Async XLA Ops:
  6.5 1.9 %copy-start = (bf16[2048,768]{1,0:T(8,128)(2,1)S(1)}, bf16[2048,768]{1,0:T(8,128)(2,1)}, u32[]{:S(2)}) copy-start(bf16[2048,768]{1,0:T(8,128)(2,1)} %param.8) | copy-start | bytes 9437188
  6.5 20.9 %copy-start.3 = (s32[1,2]{1,0:T(1,128)S(1)}, s32[1,2]{1,0:T(1,128)}, u32[]{:S(2)}) copy-start(s32[1,2]{1,0:T(1,128)} %param.11) | copy-start | bytes 28
  6.5 21.0 %copy-start.2 = (s32[1,2,2]{2,1,0:T(2,128)S(1)}, s32[1,2,2]{2,1,0:T(2,128)}, u32[]{:S(2)}) copy-start(s32[1,2,2]{2,1,0:T(2,128)} %param.10) | copy-start | bytes 52
  6.5 41.6 %all-gather.5.cloned.1.call-start = ((), (), s32[]{:S(2)}) async-start(), calls=%async_computation.1 | async-start | bytes 1310720 | tf_op jit(solution)/shard_map/all_gather | solution.py:93
  18.6 58.6 %all-gather.3.cloned.1.call-start = ((), (), s32[]{:S(2)}) async-start(), calls=%async_computation | async-start | bytes 1310720 | tf_op jit(solution)/shard_map/all_gather | solution.py:92
  18.6 5.3 %collective-permute-start = (bf16[1,256,256]{2,1,0:T(8,128)(2,1)}, bf16[1,256,256]{2,1,0:T(8,128)(2,1)}, u32[]{:S(2)}, u32[]{:S(2)}) collective-permute-start(bf16[1,256,256]{2,1,0:T(8,128)(2,1)} %get-tuple-element.37), channel_id=1, source_target_pairs={{0,1},{1,0},{2,3},{3,2},{4,5},{5,4},{6,7},{7,6},{8,9},{9,8},{10,11... | collective-permute-start | bytes 393224 | tf_op jit(solution)/shard_map/ppermute | solution.py:20
  81.4 4.2 %copy-start.1 = (bf16[2048,256]{0,1:T(8,128)(2,1)S(1)}, bf16[2048,256]{0,1:T(8,128)(2,1)}, u32[]{:S(2)}) copy-start(bf16[2048,256]{0,1:T(8,128)(2,1)} %copy.11) | copy-start | bytes 3145732 | tf_op jit(solution)/shard_map/cond
Sparse Core Ops, SparseCore 0:
  18.7 29.4 all-gather.4
  49.7 27.3 all-gather.2
